TPU v7x, 32 devices: a whole 2x2x4 slice. The times are simulated.
32 devices in a mesh: outer: 4 (over z), inner: 2 (over x), head: 4 (over y, core).
Axes of the slice: x: 2, y: 2, z: 4, core: 2. Of those that a mesh axis runs over, the one named last changes fastest.
Arguments:
- queries: bfloat16 [1024, 4096], P(('outer', 'inner'), 'head'), may hold values from -6 to 6
- keys: bfloat16 [1024, 512], P(('outer', 'inner'), 'head'), may hold values from -6 to 6
- values: bfloat16 [1024, 512], P(('outer', 'inner'), 'head'), may hold values from -6 to 6
- doc_start: int32 [1024], P(('outer', 'inner')), may hold values from 0 to 1023, as said below
- w_out: bfloat16 [4096, 4096], P('head'), may hold values from -0.09375 to 0.09375
Outputs:
- block_out: bfloat16 [1024, 4096], P(('outer', 'inner'))
Inputs may be any that keep to these rules, and one draw needn't show every extreme that they name: doc_start[t] is the first position of the document that holds token t: it never falls, doc_start[t] <= t, it equals t where a document begins, and documents hold 1 to 512 tokens, at least one exactly 512; the last token begins a document of its own.
All inputs are finite; a program needn't handle non-finite values.
Results may differ from a plain program's by a relative error of at most 0.01.
Values may be sent and summed in bfloat16 or wider, within the bound.
A program may use at most 64 MiB of HBM per device.

v0:
```python
import jax
import jax.numpy as jnp
from jax import lax
from jax.sharding import PartitionSpec as P

HEAD_SIZE = 128


masked_fill = -1e30


def from_behind(value, axis, steps):
    count = lax.axis_size(axis)
    initial, last = (max(0, -steps), min(count, count - steps))
    return lax.ppermute(value, axis, [(source, source + steps) for source in range(initial, last)])


def shards(queries, keys, values, doc_start, w_out):
    tok_rows = queries.shape[0]
    inner_count = lax.axis_size("inner")
    outer_count = lax.axis_size("outer")
    reach = min(8, outer_count // 2)
    group_len = tok_rows * inner_count
    kv_heads = keys.shape[1] // HEAD_SIZE
    q_heads = queries.shape[1] // HEAD_SIZE
    head_portion = q_heads // kv_heads
    scale = HEAD_SIZE ** (-0.5)
    outer_at = lax.axis_index("outer")
    start_pos = (outer_at * inner_count + lax.axis_index("inner")) * tok_rows
    query_pos = start_pos + jnp.arange(tok_rows, dtype=jnp.int32)
    grouped = queries.reshape(tok_rows, kv_heads, head_portion, HEAD_SIZE)

    def attend(state, block_keys, block_values, key_first):
        peak, total, accum = state
        key_matrix = block_keys.reshape(group_len, kv_heads, HEAD_SIZE)
        value_matrix = block_values.reshape(group_len, kv_heads, HEAD_SIZE)
        scores = (
            jnp.einsum("tkgd,skd->kgts", grouped, key_matrix, preferred_element_type=jnp.float32)
            * scale
        )
        key_pos = key_first + jnp.arange(group_len, dtype=jnp.int32)
        visible = (key_pos[None, :] >= doc_start[:, None]) & (
            key_pos[None, :] <= query_pos[:, None]
        )
        masked = jnp.where(visible, scores, masked_fill)
        new_peak = jnp.maximum(peak, jnp.max(masked, axis=-1))
        weights = jnp.where(visible, jnp.exp(masked - new_peak[..., None]), 0.0)
        fade = jnp.exp(peak - new_peak)
        total = total * fade + jnp.sum(weights, axis=-1)
        rounded = weights.astype(jnp.bfloat16)
        accum = accum * fade[..., None] + jnp.einsum(
            "kgts,skd->kgtd", rounded, value_matrix, preferred_element_type=jnp.float32
        )
        return (new_peak, total, accum)

    def visit(state, block_keys, block_values, key_first):
        return attend(state, block_keys, block_values, key_first)

    group_keys, group_values = (
        lax.all_gather(keys, "inner", axis=0, tiled=True),
        lax.all_gather(values, "inner", axis=0, tiled=True),
    )
    state = (
        jnp.full((kv_heads, head_portion, tok_rows), masked_fill, jnp.float32),
        jnp.zeros((kv_heads, head_portion, tok_rows), jnp.float32),
        jnp.zeros((kv_heads, head_portion, tok_rows, HEAD_SIZE), jnp.float32),
    )
    state = visit(state, group_keys, group_values, outer_at * group_len)
    for offset in range(1, reach + 1):
        far_keys, far_values = from_behind((group_keys, group_values), "outer", offset)
        state = visit(state, far_keys, far_values, (outer_at - offset) * group_len)
    peak, total, accum = state
    attended = (
        (accum / total[..., None])
        .transpose(2, 0, 1, 3)
        .reshape(tok_rows, q_heads * HEAD_SIZE)
        .astype(jnp.bfloat16)
    )
    partial_value = jnp.dot(attended, w_out, preferred_element_type=jnp.float32)
    summed = lax.psum(partial_value.astype(jnp.bfloat16), "head")
    return summed


def solution(mesh):
    placed = (
        P(("outer", "inner"), "head"),
        P(("outer", "inner"), "head"),
        P(("outer", "inner"), "head"),
        P(("outer", "inner")),
        P("head", None),
    )
    return jax.shard_map(
        shards, mesh=mesh, in_specs=placed, out_specs=P(("outer", "inner"), None), check_vma=False
    )
```

profile of v0, /device:TPU:0, one launch (start us, length us, event | category | flops | bytes accessed | tf_op | source)
XLA Modules:
  0.0 79.4 jit_solution(9427432702387886575)
XLA Ops:
  6.5 0.0 copy-start
  6.5 0.0 all-reduce.2.cloned.1.call-start
  6.5 5.9 %all_gather.6 = bf16[256,128]{1,0:T(8,128)(2,1)S(1)} all-gather(bf16[128,128]{1,0:T(8,128)(2,1)} %param.6), channel_id=1, replica_groups=mesh['outer'=4,'inner'=2,'head'=4] {'inner'}, dimensions={0}, use_global_device_ids=true | all-gather | bytes 98304 | tf_op jit(solution)/shard_map/all_gather | solution.py:60
  12.4 4.0 %collective-permute-start = (bf16[256,128]{1,0:T(8,128)(2,1)S(1)}, bf16[256,128]{1,0:T(8,128)(2,1)S(1)}, u32[]{:S(2)}, u32[]{:S(2)}) collective-permute-start(bf16[256,128]{1,0:T(8,128)(2,1)S(1)} %all_gather.6), channel_id=1, source_target_pairs={{0,8},{8,16},{16,24},{1,9},{9,17},{17,25},{2,10},{10,18},{18,26},{... | collective-permute-start | bytes 196616 | tf_op jit(solution)/shard_map/ppermute | solution.py:15
  16.4 4.5 %collective-permute-start.2 = (bf16[256,128]{1,0:T(8,128)(2,1)S(1)}, bf16[256,128]{1,0:T(8,128)(2,1)S(1)}, u32[]{:S(2)}, u32[]{:S(2)}) collective-permute-start(bf16[256,128]{1,0:T(8,128)(2,1)S(1)} %all_gather.6), channel_id=1, source_target_pairs={{0,16},{8,24},{1,17},{9,25},{2,18},{10,26},{3,19},{11,27},{4,20},{... | collective-permute-start | bytes 196616 | tf_op jit(solution)/shard_map/ppermute | solution.py:15
  20.9 0.9 %copy.7 = bf16[128,128]{0,1:T(8,128)(2,1)S(1)} copy(bf16[128,128]{1,0:T(8,128)(2,1)} %param.7) | data formatting | bytes 65536 | tf_op args[2]
  21.8 4.6 %all_gather.7 = bf16[256,128]{0,1:T(8,128)(2,1)S(1)} all-gather(bf16[128,128]{0,1:T(8,128)(2,1)S(1)} %copy.7), channel_id=1, replica_groups=mesh['outer'=4,'inner'=2,'head'=4] {'inner'}, dimensions={0}, use_global_device_ids=true | all-gather | bytes 98304 | tf_op jit(solution)/shard_map/all_gather | solution.py:61
  26.4 1.3 %collective-permute-start.3 = (bf16[256,128]{0,1:T(8,128)(2,1)S(1)}, bf16[256,128]{0,1:T(8,128)(2,1)S(1)}, u32[]{:S(2)}, u32[]{:S(2)}) collective-permute-start(bf16[256,128]{0,1:T(8,128)(2,1)S(1)} %all_gather.7), channel_id=1, source_target_pairs={{0,16},{8,24},{1,17},{9,25},{2,18},{10,26},{3,19},{11,27},{4,20},{... | collective-permute-start | bytes 196616 | tf_op jit(solution)/shard_map/ppermute | solution.py:15
  27.7 1.3 %collective-permute-start.1 = (bf16[256,128]{0,1:T(8,128)(2,1)S(1)}, bf16[256,128]{0,1:T(8,128)(2,1)S(1)}, u32[]{:S(2)}, u32[]{:S(2)}) collective-permute-start(bf16[256,128]{0,1:T(8,128)(2,1)S(1)} %all_gather.7), channel_id=1, source_target_pairs={{0,8},{8,16},{16,24},{1,9},{9,17},{17,25},{2,10},{10,18},{18,26},{... | collective-permute-start | bytes 196616 | tf_op jit(solution)/shard_map/ppermute | solution.py:15
  29.0 0.0 copy-start.1
  29.1 1.0 %compare_and_fusion.2 = (pred[128,256]{0,1:T(8,128)(4,1)S(1)}, pred[128,256]{0,1:T(8,128)(4,1)S(1)}, pred[128,256]{0,1:T(8,128)(4,1)S(1)}) fusion(s32[128]{0:T(128)S(1)} %iota_add_fusion.3, s32[128]{0:T(128)} %param.8, s32[256]{0:T(256)S(1)} %iota_add_fusion.2, s32[256]{0:T(256)S(1)} %iota_add_fusion.1, s32[256]{0:T(256)S(1)} %iota_add_fusion), kind=kLoop, calls=%fused_computation.47 | loop fusion | flops 294912 | bytes 102400 | tf_op jit(solution)/shard_map/and | solution.py:42
  30.0 0.0 copy-done
  30.1 0.3 fusion.53
  30.4 0.0 collective-permute-done
  30.4 0.3 fusion.52
  30.7 0.0 collective-permute-done.2
  30.7 0.3 fusion.51
  31.0 0.2 fusion.15
  31.2 0.4 fusion.11
  31.7 0.3 fusion.9
  32.0 0.0 collective-permute-done.3
  32.0 0.3 fusion.18
  32.3 0.0 collective-permute-done.1
  32.3 0.3 fusion.10
  32.7 0.0 copy-done.1
  32.7 2.3 %convolution_convert_fusion = bf16[128,4096]{1,0:T(8,128)(2,1)} fusion(bf16[128,1024]{0,1:T(8,128)(2,1)S(1)} %bitcast.81, bf16[1024,4096]{1,0:T(8,128)(2,1)S(1)} %copy-done.1), kind=kOutput, calls=%fused_computation | convolution fusion | flops 1074266112 | bytes 9699328 | tf_op jit(solution)/shard_map/dot_general | solution.py:79
  35.0 0.0 all-reduce.2.cloned.1.call-update
  35.0 35.3 %all-reduce.2.cloned.1.call-done = bf16[128,4096]{1,0:T(8,128)(2,1)} async-done(((bf16[128,4096]{1,0:T(8,128)(2,1)}), bf16[128,4096]{1,0:T(8,128)(2,1)}) %all-reduce.2.cloned.1.call-update) | async-done | bytes 1048592 | tf_op jit(solution)/shard_map/psum | solution.py:80
  70.3 2.3 %copy.36 = bf16[128,4096]{1,0:T(8,128)(2,1)} copy(bf16[128,4096]{1,0:T(8,128)(2,1)} %all-reduce.2.cloned.1.call-done) | data formatting | bytes 2097152
  (6 shorter events, 0.0 us)
Async XLA Ops:
  6.5 23.5 %copy-start = (bf16[128,1024]{1,0:T(8,128)(2,1)S(1)}, bf16[128,1024]{1,0:T(8,128)(2,1)}, u32[]{:S(2)}) copy-start(bf16[128,1024]{1,0:T(8,128)(2,1)} %param.5) | copy-start | bytes 786436
  6.5 63.7 %all-reduce.2.cloned.1.call-start = ((), (), s32[]{:S(2)}) async-start(), calls=%async_computation | async-start | bytes 2097152 | tf_op jit(solution)/shard_map/psum | solution.py:80
  12.4 17.9 %collective-permute-start = (bf16[256,128]{1,0:T(8,128)(2,1)S(1)}, bf16[256,128]{1,0:T(8,128)(2,1)S(1)}, u32[]{:S(2)}, u32[]{:S(2)}) collective-permute-start(bf16[256,128]{1,0:T(8,128)(2,1)S(1)} %all_gather.6), channel_id=1, source_target_pairs={{0,8},{8,16},{16,24},{1,9},{9,17},{17,25},{2,10},{10,18},{18,26},{... | collective-permute-start | bytes 196616 | tf_op jit(solution)/shard_map/ppermute | solution.py:15
  16.4 14.3 %collective-permute-start.2 = (bf16[256,128]{1,0:T(8,128)(2,1)S(1)}, bf16[256,128]{1,0:T(8,128)(2,1)S(1)}, u32[]{:S(2)}, u32[]{:S(2)}) collective-permute-start(bf16[256,128]{1,0:T(8,128)(2,1)S(1)} %all_gather.6), channel_id=1, source_target_pairs={{0,16},{8,24},{1,17},{9,25},{2,18},{10,26},{3,19},{11,27},{4,20},{... | collective-permute-start | bytes 196616 | tf_op jit(solution)/shard_map/ppermute | solution.py:15
  26.4 5.6 %collective-permute-start.3 = (bf16[256,128]{0,1:T(8,128)(2,1)S(1)}, bf16[256,128]{0,1:T(8,128)(2,1)S(1)}, u32[]{:S(2)}, u32[]{:S(2)}) collective-permute-start(bf16[256,128]{0,1:T(8,128)(2,1)S(1)} %all_gather.7), channel_id=1, source_target_pairs={{0,16},{8,24},{1,17},{9,25},{2,18},{10,26},{3,19},{11,27},{4,20},{... | collective-permute-start | bytes 196616 | tf_op jit(solution)/shard_map/ppermute | solution.py:15
  27.7 4.6 %collective-permute-start.1 = (bf16[256,128]{0,1:T(8,128)(2,1)S(1)}, bf16[256,128]{0,1:T(8,128)(2,1)S(1)}, u32[]{:S(2)}, u32[]{:S(2)}) collective-permute-start(bf16[256,128]{0,1:T(8,128)(2,1)S(1)} %all_gather.7), channel_id=1, source_target_pairs={{0,8},{8,16},{16,24},{1,9},{9,17},{17,25},{2,10},{10,18},{18,26},{... | collective-permute-start | bytes 196616 | tf_op jit(solution)/shard_map/ppermute | solution.py:15
  29.0 3.7 %copy-start.1 = (bf16[1024,4096]{1,0:T(8,128)(2,1)S(1)}, bf16[1024,4096]{1,0:T(8,128)(2,1)}, u32[]{:S(2)}) copy-start(bf16[1024,4096]{1,0:T(8,128)(2,1)} %param.9) | copy-start | bytes 25165828
Sparse Core Ops, SparseCore 0:
  35.1 35.1 all-reduce.1
where the time goes:
time: 79.7 us; the launch traced here: 79.4 us
  waiting for transfers between devices  35.3 us (44%)
  between operations  13.6 us (17%)
  starting transfers between devices  11 us (14%)
  blocking collectives  10.5 us (13%)
  matrix products  4.18 us (5%)
  local copies, waits for them, and re-layouts  3.16 us (4%)
  other arithmetic  1.6 us (2%)
    psum x1, waiting for transfers between devices, shards(): summed = lax.psum(partial_value.astype(jnp.bfloat16), 'head')  35.3 us
    ppermute x4, starting transfers between devices, from_behind(): lax.ppermute(value, axis, [(source, source + steps) for source in range(i...  11 us
    all_gather x1, blocking collectives, shards(): lax.all_gather(keys, 'inner', axis=0, tiled=True)  5.91 us
    all_gather x1, blocking collectives, shards(): lax.all_gather(values, 'inner', axis=0, tiled=True)  4.61 us
    unnamed x6, local copies, waits for them, and re-layouts  3.16 us
    dot_general x1, matrix products, shards(): partial_value = jnp.dot(attended, w_out, preferred_element_type=jnp.float32)  2.26 us
  transfers between devices with their start and end apart: 5, of which 1 were waited for; matrix products, arithmetic and copies ran while one was open for 5% of the time, Pallas kernels for 0%

commit v1 on v0

v1 whole, which is shorter than its diff:
```python
import functools
import math

import jax
import jax.numpy as jnp
from jax import lax
from jax.experimental import pallas as pl
from jax.experimental.pallas import tpu as pltpu
from jax.sharding import PartitionSpec as P

HEAD_SIZE = 128
CHUNK = 256
masked_fill = -1e30
MESH = pl.DeviceIdType.MESH


def kernel(
    n_outer, n_inner, reach,
    q_hbm, k_hbm, v_hbm, ds_hbm, w_hbm, out_ref,
    q_v, ds_v, kbuf, vbuf, wbuf, m_ref, l_ref, acc, att,
    p_other, p_own, p_recv, a_own, a_recv, y_recv, y_pair,
    local_sem, w_sem, kv_recv, z_send, x_send,
    pair_s, pair_r, ypush_s, ypush_r, asum_s, asum_r, relay_s, relay_r,
):
    tok = q_hbm.shape[0]
    heads = q_hbm.shape[1] // HEAD_SIZE
    half = w_hbm.shape[1] // 2
    n_chunk = half // CHUNK
    group_len = tok * n_inner
    o = lax.axis_index("outer")
    i = lax.axis_index("inner")
    h = lax.axis_index("head")
    side = lax.rem(h, 2)
    pair_h = h + 1 - 2 * side
    y_h = lax.rem(h + 2, 4)
    pair_dev = (o, i, pair_h)
    y_dev = (o, i, y_h)

    loads = [
        pltpu.make_async_copy(q_hbm, q_v, local_sem.at[0]),
        pltpu.make_async_copy(ds_hbm, ds_v, local_sem.at[1]),
        pltpu.make_async_copy(k_hbm, kbuf.at[0, i], local_sem.at[2]),
        pltpu.make_async_copy(v_hbm, vbuf.at[0, i], local_sem.at[3]),
    ]
    for load in loads:
        load.start()
    own_col = side * half
    other_col = (1 - side) * half
    w_loads = []
    for c in range(n_chunk):
        for which, base in ((0, other_col), (1, own_col)):
            col = pl.multiple_of(base + c * CHUNK, CHUNK)
            w_loads.append(
                pltpu.make_async_copy(
                    w_hbm.at[:, pl.ds(col, CHUNK)], wbuf.at[2 * c + which], w_sem.at[2 * c + which]
                )
            )

    def used(d, j):
        ok = o >= d
        if d == 0:
            ok = ok & (j <= i)
        if d == reach:
            ok = ok & (j >= i)
        return ok

    def sends_x(d, j):
        ok = o >= d
        if d == 0:
            ok = ok & (j > i)
        if d == reach:
            ok = ok & (j < i)
        return ok

    zeros = jnp.zeros((tok, HEAD_SIZE), jnp.bfloat16)
    for d in range(reach + 1):
        for r in range(n_inner):
            if d == 0 and r == 0:
                continue
            j = lax.rem(i + r, n_inner)

            @pl.when(jnp.logical_not(used(d, j)))
            def _(d=d, j=j):
                kbuf[d, j] = zeros
                vbuf[d, j] = zeros

    barrier = pltpu.get_barrier_semaphore()
    for peer in (pair_dev, y_dev):
        pl.semaphore_signal(barrier, inc=1, device_id=peer, device_id_type=MESH)
    for r in range(1, n_inner):
        pl.semaphore_signal(
            barrier, inc=1, device_id=(o, lax.rem(i + r, n_inner), h), device_id_type=MESH
        )

    @pl.when(o > 0)
    def _():
        pl.semaphore_signal(barrier, inc=1, device_id=(o - 1, i, h), device_id_type=MESH)

    @pl.when(o < n_outer - 1)
    def _():
        pl.semaphore_signal(barrier, inc=1, device_id=(o + 1, i, h), device_id_type=MESH)

    behind = jnp.where(o > 0, 1, 0)
    ahead = jnp.where(o < n_outer - 1, 1, 0)
    pl.semaphore_wait(barrier, 1 + n_inner + behind + ahead)

    bufs = (kbuf, vbuf)
    hbms = (k_hbm, v_hbm)

    def z_copy(t, d):
        src = hbms[t] if d == 0 else bufs[t].at[d, i]
        return pltpu.make_async_remote_copy(
            src_ref=src, dst_ref=bufs[t].at[d + 1, i],
            send_sem=z_send.at[t, d], recv_sem=kv_recv.at[t, d + 1, i],
            device_id=(o + 1, i, h), device_id_type=MESH,
        )

    def x_copy(t, d, r):
        src = hbms[t] if d == 0 else bufs[t].at[d, i]
        return pltpu.make_async_remote_copy(
            src_ref=src, dst_ref=bufs[t].at[d, i],
            send_sem=x_send.at[t, d, r], recv_sem=kv_recv.at[t, d, i],
            device_id=(o, lax.rem(i + r, n_inner), h), device_id_type=MESH,
        )

    def arrival(t, d, j):
        return pltpu.make_async_remote_copy(
            src_ref=bufs[t].at[d, j], dst_ref=bufs[t].at[d, j],
            send_sem=z_send.at[t, 0], recv_sem=kv_recv.at[t, d, j],
            device_id=(o, lax.rem(i + 1, n_inner), h), device_id_type=MESH,
        )

    def z_ok(d):
        return (o >= d) & (o < n_outer - 1)

    def forward(t, d):
        if d < reach:
            @pl.when(z_ok(d))
            def _():
                z_copy(t, d).start()
        for r in range(1, n_inner):
            @pl.when(sends_x(d, lax.rem(i + r, n_inner)))
            def _():
                x_copy(t, d, r).start()

    for t in range(2):
        forward(t, 0)
    for w_load in w_loads:
        w_load.start()

    coef = HEAD_SIZE ** (-0.5) * math.log2(math.e)
    start_pos = (o * n_inner + i) * tok

    def visit(d):
        for r in range(1, n_inner):
            j = lax.rem(i + r, n_inner)

            @pl.when(used(d, j))
            def _():
                for t in range(2):
                    arrival(t, d, j).wait_recv()
        k = kbuf[d].reshape(group_len, HEAD_SIZE)
        v_t = vbuf[d].reshape(group_len, HEAD_SIZE).T
        key_pos = (o - d) * group_len + lax.broadcasted_iota(jnp.int32, (group_len, tok), 0)
        query_pos = start_pos + lax.broadcasted_iota(jnp.int32, (group_len, tok), 1)
        starts = ds_v[...].reshape(1, tok)
        visible = (key_pos >= starts) & (key_pos <= query_pos)
        for g in range(heads):
            q = q_v[:, g * HEAD_SIZE:(g + 1) * HEAD_SIZE]
            s = lax.dot_general(k, q, (((1,), (1,)), ((), ())), preferred_element_type=jnp.float32)
            s = jnp.where(visible, s, masked_fill)
            top = jnp.max(s, axis=0, keepdims=True)
            if d == 0:
                peak = top
            else:
                peak = jnp.maximum(m_ref[g:g + 1], top)
                fade = jnp.exp2((m_ref[g:g + 1] - peak) * coef)
            p = jnp.exp2((s - peak) * coef)
            total = jnp.sum(p, axis=0, keepdims=True)
            mixed = jnp.dot(v_t, p.astype(jnp.bfloat16), preferred_element_type=jnp.float32)
            if d > 0:
                total = total + l_ref[g:g + 1] * fade
                mixed = mixed + acc[g] * fade
            if d < reach:
                m_ref[g:g + 1] = peak
                l_ref[g:g + 1] = total
                acc[g] = mixed
            else:
                att[:, g * HEAD_SIZE:(g + 1) * HEAD_SIZE] = (
                    (mixed * (1.0 / total)).T.astype(jnp.bfloat16)
                )

    for load in loads:
        load.wait()
    for d in range(1, reach + 1):
        for t in range(2):
            @pl.when(o >= d)
            def _():
                arrival(t, d, i).wait_recv()
            forward(t, d)
        visit(d - 1)
    visit(reach)

    def to_pair(c):
        return pltpu.make_async_remote_copy(
            src_ref=p_other.at[c], dst_ref=p_recv.at[c],
            send_sem=pair_s.at[c], recv_sem=pair_r.at[c],
            device_id=pair_dev, device_id_type=MESH,
        )

    def to_y(c):
        return pltpu.make_async_remote_copy(
            src_ref=a_own.at[c], dst_ref=y_recv.at[c],
            send_sem=ypush_s.at[c], recv_sem=ypush_r.at[c],
            device_id=y_dev, device_id_type=MESH,
        )

    def sum_to_pair(c):
        return pltpu.make_async_remote_copy(
            src_ref=a_own.at[c], dst_ref=a_recv.at[c],
            send_sem=asum_s.at[c], recv_sem=asum_r.at[c],
            device_id=pair_dev, device_id_type=MESH,
        )

    def relay(c):
        return pltpu.make_async_remote_copy(
            src_ref=y_recv.at[c], dst_ref=y_pair.at[c],
            send_sem=relay_s.at[c], recv_sem=relay_r.at[c],
            device_id=pair_dev, device_id_type=MESH,
        )

    def product(slot):
        w_loads[slot].wait()
        return jnp.dot(att[...], wbuf[slot], preferred_element_type=jnp.float32).astype(jnp.bfloat16)

    def join(c):
        to_pair(c).wait_recv()
        a_own[c] = (
            p_own[c].astype(jnp.float32) + p_recv[c].astype(jnp.float32)
        ).astype(jnp.bfloat16)
        to_y(c).start()
        sum_to_pair(c).start()

    for c in range(n_chunk):
        p_other[c] = product(2 * c)
        to_pair(c).start()
        p_own[c] = product(2 * c + 1)
        if c >= 1:
            join(c - 1)
    join(n_chunk - 1)

    def finish(c):
        sum_to_pair(c).wait_recv()
        relay(c).wait_recv()
        col = pl.multiple_of(other_col + c * CHUNK, CHUNK)
        out_ref[:, pl.ds(col, CHUNK)] = (
            a_recv[c].astype(jnp.float32) + y_pair[c].astype(jnp.float32)
        ).astype(jnp.bfloat16)

    for c in range(n_chunk):
        to_y(c).wait_recv()
        relay(c).start()
        col = pl.multiple_of(own_col + c * CHUNK, CHUNK)
        out_ref[:, pl.ds(col, CHUNK)] = (
            a_own[c].astype(jnp.float32) + y_recv[c].astype(jnp.float32)
        ).astype(jnp.bfloat16)
        if c >= 1:
            finish(c - 1)
    finish(n_chunk - 1)

    for t in range(2):
        for d in range(reach + 1):
            if d < reach:
                @pl.when(z_ok(d))
                def _():
                    z_copy(t, d).wait_send()
            for r in range(1, n_inner):
                @pl.when(sends_x(d, lax.rem(i + r, n_inner)))
                def _():
                    x_copy(t, d, r).wait_send()
    for c in range(n_chunk):
        to_pair(c).wait_send()
        to_y(c).wait_send()
        sum_to_pair(c).wait_send()
        relay(c).wait_send()


def shards(n_outer, n_inner, queries, keys, values, doc_start, w_out):
    tok = queries.shape[0]
    heads = queries.shape[1] // HEAD_SIZE
    dout = w_out.shape[1]
    reach = min(8, n_outer // 2)
    n_chunk = dout // 2 // CHUNK
    bf16, f32 = jnp.bfloat16, jnp.float32
    dma = pltpu.SemaphoreType.DMA
    slots = (reach + 1, n_inner, tok, HEAD_SIZE)
    piece = pltpu.VMEM((n_chunk, tok, CHUNK), bf16)
    any_spec = pl.BlockSpec(memory_space=pltpu.HBM)
    return pl.pallas_call(
        functools.partial(kernel, n_outer, n_inner, reach),
        out_shape=jax.ShapeDtypeStruct((tok, dout), bf16),
        in_specs=[any_spec] * 5,
        out_specs=pl.BlockSpec(memory_space=pltpu.VMEM),
        scratch_shapes=[
            pltpu.VMEM(queries.shape, bf16),
            pltpu.VMEM((tok,), jnp.int32),
            pltpu.VMEM(slots, bf16),
            pltpu.VMEM(slots, bf16),
            pltpu.VMEM((2 * n_chunk, w_out.shape[0], CHUNK), bf16),
            pltpu.VMEM((heads, tok), f32),
            pltpu.VMEM((heads, tok), f32),
            pltpu.VMEM((heads, HEAD_SIZE, tok), f32),
            pltpu.VMEM((tok, heads * HEAD_SIZE), bf16),
            piece, piece, piece, piece, piece, piece, piece,
            dma((4,)),
            dma((2 * n_chunk,)),
            dma((2, reach + 1, n_inner)),
            dma((2, reach)),
            dma((2, reach + 1, n_inner)),
        ] + [dma((n_chunk,))] * 8,
        compiler_params=pltpu.CompilerParams(
            collective_id=0, has_side_effects=True, vmem_limit_bytes=67043328
        ),
    )(queries, keys, values, doc_start, w_out)


def solution(mesh):
    placed = (
        P(("outer", "inner"), "head"),
        P(("outer", "inner"), "head"),
        P(("outer", "inner"), "head"),
        P(("outer", "inner")),
        P("head", None),
    )
    body = functools.partial(shards, mesh.shape["outer"], mesh.shape["inner"])
    return jax.shard_map(
        body, mesh=mesh, in_specs=placed, out_specs=P(("outer", "inner"), None), check_vma=False
    )
```

time: 79.7 us -> 32.4 us (0.41)
  the two profiles are of different devices: /device:TPU:0 before, /device:TPU:25 now
where the time goes in v1:
time: 32.4 us; the launch traced here: 32.3 us
  Pallas kernels  30 us (93%)
  local copies, waits for them, and re-layouts  2.29 us (7%)
    pallas_call x1, Pallas kernels, shards(): pl.pallas_call(functools.partial(kernel, n_outer, n_inner, reach), out_sh...  30 us
    unnamed x1, local copies, waits for them, and re-layouts  2.29 us

profile of v1, /device:TPU:25, one launch (start us, length us, event | category | flops | bytes accessed | tf_op | source)
XLA Modules:
  0.0 32.3 jit_solution(3140655278161963583)
XLA Ops:
  0.0 30.0 %shard_map.55 = bf16[128,4096]{1,0:T(8,128)(2,1)} custom-call(bf16[128,1024]{1,0:T(8,128)(2,1)} %q_hbm.1, bf16[128,128]{1,0:T(8,128)(2,1)} %k_hbm.1, bf16[128,128]{1,0:T(8,128)(2,1)} %v_hbm.1, s32[128]{0:T(128)} %ds_hbm.1, bf16[1024,4096]{1,0:T(8,128)(2,1)} %w_hbm.1), custom_call_target="tpu_custom_call" | custom-call | tf_op jit(solution)/shard_map/pallas_call | solution.py:299
  30.0 2.3 %copy.7 = bf16[128,4096]{1,0:T(8,128)(2,1)} copy(bf16[128,4096]{1,0:T(8,128)(2,1)} %shard_map.55) | data formatting | bytes 2097152

commit v2 on v1

--- a/solution.py
+++ b/solution.py
@@ -298,7 +298,7 @@
     any_spec = pl.BlockSpec(memory_space=pltpu.HBM)
     return pl.pallas_call(
         functools.partial(kernel, n_outer, n_inner, reach),
-        out_shape=jax.ShapeDtypeStruct((tok, dout), bf16),
+        out_shape=pltpu.VMEM((tok, dout), bf16),
         in_specs=[any_spec] * 5,
         out_specs=pl.BlockSpec(memory_space=pltpu.VMEM),
         scratch_shapes=[
@@ -319,7 +319,7 @@
             dma((2, reach + 1, n_inner)),
         ] + [dma((n_chunk,))] * 8,
         compiler_params=pltpu.CompilerParams(
-            collective_id=0, has_side_effects=True, vmem_limit_bytes=67043328
+            collective_id=0, has_side_effects=True, vmem_limit_bytes=60 * 1024 * 1024
         ),
     )(queries, keys, values, doc_start, w_out)
 

time: 32.4 us -> 30.1 us (0.929)
  local copies, waits for them, and re-layouts: 2.29 us -> 0.97 us
  Pallas kernels: 30 us -> 29 us
    unnamed x1, local copies, waits for them, and re-layouts: 2.29 us -> 0.97 us
    pallas_call x1, Pallas kernels: 30 us -> 29 us  [shards(): pl.pallas_call(functools.partial(kernel, n_outer, n_inner, reach), out_sh...]
where the time goes in v2:
time: 30.1 us; the launch traced here: 30 us
  Pallas kernels  29 us (96%)
  local copies, waits for them, and re-layouts  0.97 us (3%)
    pallas_call x1, Pallas kernels, shards(): pl.pallas_call(functools.partial(kernel, n_outer, n_inner, reach), out_sh...  29 us
    unnamed x1, local copies, waits for them, and re-layouts  0.97 us

profile of v2, /device:TPU:25, one launch (start us, length us, event | category | flops | bytes accessed | tf_op | source)
XLA Modules:
  0.0 30.0 jit_solution(15554350696673943302)
XLA Ops:
  0.0 29.0 %shard_map.55 = bf16[128,4096]{1,0:T(8,128)(2,1)S(1)} custom-call(bf16[128,1024]{1,0:T(8,128)(2,1)} %q_hbm.1, bf16[128,128]{1,0:T(8,128)(2,1)} %k_hbm.1, bf16[128,128]{1,0:T(8,128)(2,1)} %v_hbm.1, s32[128]{0:T(128)} %ds_hbm.1, bf16[1024,4096]{1,0:T(8,128)(2,1)} %w_hbm.1), custom_call_target="tpu_custom_call" | custom-call | tf_op jit(solution)/shard_map/pallas_call | solution.py:299
  29.0 1.0 %copy.7 = bf16[128,4096]{1,0:T(8,128)(2,1)} copy(bf16[128,4096]{1,0:T(8,128)(2,1)S(1)} %shard_map.55) | data formatting | bytes 2097152

commit v3 on v2

--- a/solution.py
+++ b/solution.py
@@ -10,6 +10,7 @@
 
 HEAD_SIZE = 128
 CHUNK = 256
+PIECES = 1
 masked_fill = -1e30
 MESH = pl.DeviceIdType.MESH
 
@@ -102,51 +103,54 @@
 
     behind = jnp.where(o > 0, 1, 0)
     ahead = jnp.where(o < n_outer - 1, 1, 0)
+    for load in loads:
+        load.wait()
     pl.semaphore_wait(barrier, 1 + n_inner + behind + ahead)
 
     bufs = (kbuf, vbuf)
-    hbms = (k_hbm, v_hbm)
-
-    def z_copy(t, d):
-        src = hbms[t] if d == 0 else bufs[t].at[d, i]
-        return pltpu.make_async_remote_copy(
-            src_ref=src, dst_ref=bufs[t].at[d + 1, i],
-            send_sem=z_send.at[t, d], recv_sem=kv_recv.at[t, d + 1, i],
+
+    rows = tok // PIECES
+
+    def part(t, d, j, p):
+        return bufs[t].at[d, j, pl.ds(p * rows, rows)]
+
+    def z_copy(t, d, p):
+        return pltpu.make_async_remote_copy(
+            src_ref=part(t, d, i, p), dst_ref=part(t, d + 1, i, p),
+            send_sem=z_send.at[t, d, p], recv_sem=kv_recv.at[t, d + 1, i, p],
             device_id=(o + 1, i, h), device_id_type=MESH,
         )
 
-    def x_copy(t, d, r):
-        src = hbms[t] if d == 0 else bufs[t].at[d, i]
-        return pltpu.make_async_remote_copy(
-            src_ref=src, dst_ref=bufs[t].at[d, i],
-            send_sem=x_send.at[t, d, r], recv_sem=kv_recv.at[t, d, i],
+    def x_copy(t, d, r, p):
+        return pltpu.make_async_remote_copy(
+            src_ref=part(t, d, i, p), dst_ref=part(t, d, i, p),
+            send_sem=x_send.at[t, d, r, p], recv_sem=kv_recv.at[t, d, i, p],
             device_id=(o, lax.rem(i + r, n_inner), h), device_id_type=MESH,
         )
 
-    def arrival(t, d, j):
-        return pltpu.make_async_remote_copy(
-            src_ref=bufs[t].at[d, j], dst_ref=bufs[t].at[d, j],
-            send_sem=z_send.at[t, 0], recv_sem=kv_recv.at[t, d, j],
+    def arrival(t, d, j, p):
+        return pltpu.make_async_remote_copy(
+            src_ref=part(t, d, j, p), dst_ref=part(t, d, j, p),
+            send_sem=z_send.at[t, 0, p], recv_sem=kv_recv.at[t, d, j, p],
             device_id=(o, lax.rem(i + 1, n_inner), h), device_id_type=MESH,
         )
 
     def z_ok(d):
         return (o >= d) & (o < n_outer - 1)
 
-    def forward(t, d):
+    def forward(t, d, p):
         if d < reach:
             @pl.when(z_ok(d))
             def _():
-                z_copy(t, d).start()
+                z_copy(t, d, p).start()
         for r in range(1, n_inner):
             @pl.when(sends_x(d, lax.rem(i + r, n_inner)))
             def _():
-                x_copy(t, d, r).start()
+                x_copy(t, d, r, p).start()
 
     for t in range(2):
-        forward(t, 0)
-    for w_load in w_loads:
-        w_load.start()
+        for p in range(PIECES):
+            forward(t, 0, p)
 
     coef = HEAD_SIZE ** (-0.5) * math.log2(math.e)
     start_pos = (o * n_inner + i) * tok
@@ -158,7 +162,8 @@
             @pl.when(used(d, j))
             def _():
                 for t in range(2):
-                    arrival(t, d, j).wait_recv()
+                    for p in range(PIECES):
+                        arrival(t, d, j, p).wait_recv()
         k = kbuf[d].reshape(group_len, HEAD_SIZE)
         v_t = vbuf[d].reshape(group_len, HEAD_SIZE).T
         key_pos = (o - d) * group_len + lax.broadcasted_iota(jnp.int32, (group_len, tok), 0)
@@ -190,14 +195,16 @@
                     (mixed * (1.0 / total)).T.astype(jnp.bfloat16)
                 )
 
-    for load in loads:
-        load.wait()
     for d in range(1, reach + 1):
         for t in range(2):
-            @pl.when(o >= d)
-            def _():
-                arrival(t, d, i).wait_recv()
-            forward(t, d)
+            for p in range(PIECES):
+                @pl.when(o >= d)
+                def _():
+                    arrival(t, d, i, p).wait_recv()
+                forward(t, d, p)
+        if d == 1:
+            for w_load in w_loads:
+                w_load.start()
         visit(d - 1)
     visit(reach)
 
@@ -270,14 +277,15 @@
 
     for t in range(2):
         for d in range(reach + 1):
-            if d < reach:
-                @pl.when(z_ok(d))
-                def _():
-                    z_copy(t, d).wait_send()
-            for r in range(1, n_inner):
-                @pl.when(sends_x(d, lax.rem(i + r, n_inner)))
-                def _():
-                    x_copy(t, d, r).wait_send()
+            for p in range(PIECES):
+                if d < reach:
+                    @pl.when(z_ok(d))
+                    def _():
+                        z_copy(t, d, p).wait_send()
+                for r in range(1, n_inner):
+                    @pl.when(sends_x(d, lax.rem(i + r, n_inner)))
+                    def _():
+                        x_copy(t, d, r, p).wait_send()
     for c in range(n_chunk):
         to_pair(c).wait_send()
         to_y(c).wait_send()
@@ -314,9 +322,9 @@
             piece, piece, piece, piece, piece, piece, piece,
             dma((4,)),
             dma((2 * n_chunk,)),
-            dma((2, reach + 1, n_inner)),
-            dma((2, reach)),
-            dma((2, reach + 1, n_inner)),
+            dma((2, reach + 1, n_inner, PIECES)),
+            dma((2, reach, PIECES)),
+            dma((2, reach + 1, n_inner, PIECES)),
         ] + [dma((n_chunk,))] * 8,
         compiler_params=pltpu.CompilerParams(
             collective_id=0, has_side_effects=True, vmem_limit_bytes=60 * 1024 * 1024

time: 30.1 us -> 29.9 us (level)
  no operation moved by 1% of the time
where the time goes in v3:
time: 29.9 us; the launch traced here: 29.7 us
  Pallas kernels  28.8 us (96%)
  local copies, waits for them, and re-layouts  0.97 us (3%)
    pallas_call x1, Pallas kernels, shards(): pl.pallas_call(functools.partial(kernel, n_outer, n_inner, reach), out_sh...  28.8 us
    unnamed x1, local copies, waits for them, and re-layouts  0.97 us

profile of v3, /device:TPU:25, one launch (start us, length us, event | category | flops | bytes accessed | tf_op | source)
XLA Modules:
  0.0 29.7 jit_solution(17775164039203855939)
XLA Ops:
  0.0 28.8 %shard_map.55 = bf16[128,4096]{1,0:T(8,128)(2,1)S(1)} custom-call(bf16[128,1024]{1,0:T(8,128)(2,1)} %q_hbm.1, bf16[128,128]{1,0:T(8,128)(2,1)} %k_hbm.1, bf16[128,128]{1,0:T(8,128)(2,1)} %v_hbm.1, s32[128]{0:T(128)} %ds_hbm.1, bf16[1024,4096]{1,0:T(8,128)(2,1)} %w_hbm.1), custom_call_target="tpu_custom_call" | custom-call | tf_op jit(solution)/shard_map/pallas_call | solution.py:307
  28.8 1.0 %copy.7 = bf16[128,4096]{1,0:T(8,128)(2,1)} copy(bf16[128,4096]{1,0:T(8,128)(2,1)S(1)} %shard_map.55) | data formatting | bytes 2097152
